TPU v7x, 512 devices: a whole 4x4x16 slice. The times are simulated.
512 devices in a mesh: term: 8 (over y, core), doc: 16 (over z), enc: 4 (over x).
Axes of the slice: x: 4, y: 4, z: 16, core: 2. Of those that a mesh axis runs over, the one named last changes fastest.
Arguments:
- query_weights: bfloat16 [1024, 30720], P('enc', ('term', 'doc')), may hold values from 0.049804688 to 2
- tile_terms: int32 [30720], P(('term', 'doc')), may hold values from 0 to 59
- tile_blocks: int32 [30720], P(('term', 'doc')), may hold values from 0 to 15
- tile_counts: int32 [128], P(('term', 'doc')), may hold values from 60 to 240, as said below
- impacts: bfloat16 [30720, 64, 128], P(('term', 'doc')), may hold values from -0.015625 to 0.015625
Outputs:
- scores: float32 [2048, 1024], P('doc', 'enc')
Inputs may be any that keep to these rules, and one draw needn't show every extreme that they name: Slots at positions tile_counts or later of a device's list are padding and contribute nothing; some device has all 240 slots live.
All inputs are finite; a program needn't handle non-finite values.
Results may differ from a plain program's by a relative error of at most 0.0003.
Values may be sent and summed in bfloat16 or wider, within the bound.
No kernel may reach another device: no remote copies, remote signals or barrier semaphores. Data moves between devices by JAX's collectives and lax.ppermute only.
A program may use at most 64 MiB of HBM per device.

v0:
```python
import jax
import jax.numpy as jnp
from jax import lax
from jax.sharding import PartitionSpec as P


def block_size(tiles):
    largest = 1
    for divisor in range(1, 65):
        if tiles % divisor == 0:
            largest = divisor
    return largest


def per_device(query_weights, tile_terms, tile_blocks, tile_counts, impacts):
    range_rows = lax.all_gather(query_weights, "doc", axis=1, tiled=True)
    queries = range_rows.shape[0]
    tiles, term_block, doc_block = impacts.shape
    owners = lax.axis_size("doc")
    grouped = range_rows.reshape(queries, range_rows.shape[1] // term_block, term_block)
    step = block_size(tiles)
    live = jnp.arange(tiles, dtype=jnp.int32) < tile_counts[0]
    owner_ids = jnp.arange(owners, dtype=jnp.int32)

    def accumulate(total, number):
        start = number * step
        term_now = lax.dynamic_slice_in_dim(tile_terms, start, step)
        owner_now = lax.dynamic_slice_in_dim(tile_blocks, start, step)
        keep_now = lax.dynamic_slice_in_dim(live, start, step)
        tile_now = lax.dynamic_slice_in_dim(impacts, start, step)
        picked = jnp.take(grouped, term_now, axis=1)
        product = jnp.einsum("qnk,nkd->ndq", picked, tile_now, preferred_element_type=jnp.float32)
        select = ((owner_now[:, None] == owner_ids[None, :]) & keep_now[:, None]).astype(
            jnp.float32
        )
        added = jnp.einsum("ndq,nb->bdq", product, select, precision=lax.Precision.HIGHEST)
        return (total + added, None)

    start_total = jnp.zeros((owners, doc_block, queries), jnp.float32)
    total, unused = lax.scan(accumulate, start_total, jnp.arange(tiles // step, dtype=jnp.int32))
    partial_value = total.reshape(owners * doc_block, queries)
    mine = lax.psum_scatter(partial_value, "doc", scatter_dimension=0, tiled=True)
    scores = lax.psum(mine, "term")
    return scores


def solution(mesh):
    return jax.shard_map(
        per_device,
        mesh=mesh,
        in_specs=(
            P("enc", ("term", "doc")),
            P(("term", "doc")),
            P(("term", "doc")),
            P(("term", "doc")),
            P(("term", "doc"), None, None),
        ),
        out_specs=P("doc", "enc"),
        check_vma=False,
    )
```

profile of v0, /device:TPU:2, one launch (start us, length us, event | category | flops | bytes accessed | tf_op | source)
XLA Modules:
  0.0 312.8 jit_solution(1491762189442942286)
XLA Ops:
  6.5 0.7 all-gather.2.cloned.1.call-update
  8.0 78.3 %all-gather.2.cloned.1.call-done = bf16[256,3840]{0,1:T(8,128)(2,1)} async-done(((bf16[256,240]{0,1:T(8,128)(2,1)}), bf16[256,3840]{0,1:T(8,128)(2,1)}) %all-gather.2.cloned.1.call-update) | async-done | bytes 1966096 | tf_op jit(solution)/shard_map/all_gather | solution.py:16
  86.2 67.8 %while.11 = (s32[]{:T(128)}, f32[16,128,256]{2,0,1:T(8,128)}, s32[4]{0:T(128)S(1)}, s32[240]{0:T(256)}, pred[240]{0:T(512)(128)(4,1)S(1)}, /*index=5*/bf16[240,6...) while((s32[]{:T(128)}, f32[16,128,256]{2,0,1:T(8,128)}, ...), condition=%wide.region_1.2_spmd.clone, body=%wide.region_0.1_spmd.clone.sunk | while | flops 631180544 | bytes 43587780 | solution.py:40
  86.2 0.6 dynamic_slice.30
  87.6 0.8 dynamic_slice.31
  88.3 0.8 compare_and_fusion.2
  89.1 2.2 gather_fusion
  91.3 2.6 fusion.28
  93.9 7.9 %select_add_fusion.2 = f32[16,128,256]{2,0,1:T(8,128)S(1)} fusion(f32[16,128,256]{2,0,1:T(8,128)S(1)} %copy-done, f32[60,128,256]{2,1,0:T(8,128)S(1)} %fusion.28, pred[]{:T(512)S(6)} %compare.3, s32[60]{0:T(128)S(1)} %dynamic_slice.31, pred[60]{0:T(512)(128)(4,1)S(1)} %dynamic_slice.32), kind=kOutput, calls=%fused_computation.4.clone.1 | convolution fusion | flops 378537856 | bytes 12058925 | tf_op jit(solution)/shard_map/while/body/eval_jaxpr/ndq,nb->bdq/dot_general | solution.py:36
  101.9 1.3 copy-done.1
  104.5 0.8 dynamic_slice.31
  105.2 0.8 compare_and_fusion.2
  106.0 2.2 gather_fusion
  108.3 2.6 fusion.28
  110.9 7.9 %select_add_fusion.2 = f32[16,128,256]{2,0,1:T(8,128)S(1)} fusion(f32[16,128,256]{2,0,1:T(8,128)S(1)} %copy-done, f32[60,128,256]{2,1,0:T(8,128)S(1)} %fusion.28, pred[]{:T(512)S(6)} %compare.3, s32[60]{0:T(128)S(1)} %dynamic_slice.31, pred[60]{0:T(512)(128)(4,1)S(1)} %dynamic_slice.32), kind=kOutput, calls=%fused_computation.4.clone.1 | convolution fusion | flops 378537856 | bytes 12058925 | tf_op jit(solution)/shard_map/while/body/eval_jaxpr/ndq,nb->bdq/dot_general | solution.py:36
  118.8 1.3 copy-done.1
  121.4 0.8 dynamic_slice.31
  122.2 0.8 compare_and_fusion.2
  122.9 2.2 gather_fusion
  125.2 2.6 fusion.28
  127.8 7.9 %select_add_fusion.2 = f32[16,128,256]{2,0,1:T(8,128)S(1)} fusion(f32[16,128,256]{2,0,1:T(8,128)S(1)} %copy-done, f32[60,128,256]{2,1,0:T(8,128)S(1)} %fusion.28, pred[]{:T(512)S(6)} %compare.3, s32[60]{0:T(128)S(1)} %dynamic_slice.31, pred[60]{0:T(512)(128)(4,1)S(1)} %dynamic_slice.32), kind=kOutput, calls=%fused_computation.4.clone.1 | convolution fusion | flops 378537856 | bytes 12058925 | tf_op jit(solution)/shard_map/while/body/eval_jaxpr/ndq,nb->bdq/dot_general | solution.py:36
  135.7 1.3 copy-done.1
  138.4 0.8 dynamic_slice.31
  139.1 0.8 compare_and_fusion.2
  139.9 2.2 gather_fusion
  142.1 2.6 fusion.28
  144.8 7.9 %select_add_fusion.2 = f32[16,128,256]{2,0,1:T(8,128)S(1)} fusion(f32[16,128,256]{2,0,1:T(8,128)S(1)} %copy-done, f32[60,128,256]{2,1,0:T(8,128)S(1)} %fusion.28, pred[]{:T(512)S(6)} %compare.3, s32[60]{0:T(128)S(1)} %dynamic_slice.31, pred[60]{0:T(512)(128)(4,1)S(1)} %dynamic_slice.32), kind=kOutput, calls=%fused_computation.4.clone.1 | convolution fusion | flops 378537856 | bytes 12058925 | tf_op jit(solution)/shard_map/while/body/eval_jaxpr/ndq,nb->bdq/dot_general | solution.py:36
  152.7 1.3 copy-done.1
  154.0 4.1 %copy.8 = f32[16,128,256]{2,1,0:T(8,128)} copy(f32[16,128,256]{2,0,1:T(8,128)} %get-tuple-element.52) | data formatting | bytes 4194304 | tf_op jit(solution)/shard_map/while | solution.py:40
  158.2 71.0 %reduce-scatter.2.cloned.1.call-done = f32[128,256]{1,0:T(8,128)} async-done(((f32[2048,256]{1,0:T(8,128)}), f32[128,256]{1,0:T(8,128)}) %reduce-scatter.2.cloned.1.call-update) | async-done | bytes 131088 | tf_op jit(solution)/shard_map/reduce_scatter | solution.py:42
  229.3 75.4 %all-reduce.2.cloned.1.call-done = f32[128,256]{1,0:T(8,128)} async-done(((f32[128,256]{1,0:T(8,128)}), f32[128,256]{1,0:T(8,128)}) %all-reduce.2.cloned.1.call-update) | async-done | bytes 131088 | tf_op jit(solution)/shard_map/psum | solution.py:43
  304.7 1.6 copy.24
  (31 shorter events, 2.3 us)
Async XLA Ops:
  6.5 79.7 %all-gather.2.cloned.1.call-start = ((), (), s32[]{:S(2)}) async-start(), calls=%async_computation.1 | async-start | bytes 2088960 | tf_op jit(solution)/shard_map/all_gather | solution.py:16
  7.3 222.0 %reduce-scatter.2.cloned.1.call-start = ((), (), s32[]{:S(2)}) async-start(), calls=%async_computation.2 | async-start | bytes 2228224 | tf_op jit(solution)/shard_map/reduce_scatter | solution.py:42
  91.3 2.6 copy-start
  101.8 1.3 copy-start.1
  108.2 2.6 copy-start
  118.8 1.3 copy-start.1
  125.2 2.6 copy-start
  135.7 1.3 copy-start.1
  142.1 2.6 copy-start
  152.7 1.3 copy-start.1
  158.2 146.6 %all-reduce.2.cloned.1.call-start = ((), (), s32[]{:S(2)}) async-start(), calls=%async_computation.3 | async-start | bytes 262144 | tf_op jit(solution)/shard_map/psum | solution.py:43
Sparse Core Ops, SparseCore 0:
  9.4 76.7 all-gather.1
  158.3 70.9 reduce-scatter.1
  231.6 73.0 all-reduce.1
where the time goes:
time: 313 us
  waiting for transfers between devices  225 us (72%)
  matrix products  42 us (13%)
  local copies, waits for them, and re-layouts  25.7 us (8%)
  between operations  13.8 us (4%)
    all_gather x1, waiting for transfers between devices, per_device(): range_rows = lax.all_gather(query_weights, 'doc', axis=1, tiled=True)  78.3 us
    psum x1, waiting for transfers between devices, per_device(): scores = lax.psum(mine, 'term')  75.4 us
    reduce_scatter x1, waiting for transfers between devices, per_device(): lax.psum_scatter(partial_value, 'doc', scatter_dimension=0, tiled=True)  71 us
    dot_general x4, matrix products, accumulate(): jnp.einsum('ndq,nb->bdq', product, select, precision=lax.Precision.HIGHEST)  31.6 us
    dot_general x4, matrix products, accumulate(): jnp.einsum('qnk,nkd->ndq', picked, tile_now, preferred_element_type=jnp.f...  10.5 us
    gather x4, local copies, waits for them, and re-layouts, accumulate(): picked = jnp.take(grouped, term_now, axis=1)  8.92 us
  transfers between devices with their start and end apart: 3, of which 3 were waited for; matrix products, arithmetic and copies ran while one was open for 0% of the time, Pallas kernels for 0%

commit v1 on v0

--- a/solution.py
+++ b/solution.py
@@ -40,7 +40,7 @@
     total, unused = lax.scan(accumulate, start_total, jnp.arange(tiles // step, dtype=jnp.int32))
     partial_value = total.reshape(owners * doc_block, queries)
     mine = lax.psum_scatter(partial_value, "doc", scatter_dimension=0, tiled=True)
-    scores = lax.psum(mine, "term")
+    scores = jnp.sum(lax.all_gather(mine, "term"), axis=0)
     return scores
 
 

time: 313 us -> 270 us (0.86)
  the two profiles are of different devices: /device:TPU:2 before, /device:TPU:1 now
where the time goes in v1:
time: 270 us
  waiting for transfers between devices  182 us (67%)
  matrix products  42 us (16%)
  local copies, waits for them, and re-layouts  24.1 us (9%)
  between operations  13.8 us (5%)
  other arithmetic  5.01 us (2%)
  loops' own time  2.71 us (1%)
    reduce_scatter x1, waiting for transfers between devices, per_device(): lax.psum_scatter(partial_value, 'doc', scatter_dimension=0, tiled=True)  69.9 us
    all_gather x1, waiting for transfers between devices, per_device(): range_rows = lax.all_gather(query_weights, 'doc', axis=1, tiled=True)  69.7 us
    all_gather x1, waiting for transfers between devices, per_device(): scores = jnp.sum(lax.all_gather(mine, 'term'), axis=0)  41.8 us
    dot_general x4, matrix products, accumulate(): jnp.einsum('ndq,nb->bdq', product, select, precision=lax.Precision.HIGHEST)  31.6 us
    dot_general x4, matrix products, accumulate(): jnp.einsum('qnk,nkd->ndq', picked, tile_now, preferred_element_type=jnp.f...  10.5 us
    gather x4, local copies, waits for them, and re-layouts, accumulate(): picked = jnp.take(grouped, term_now, axis=1)  8.92 us
  transfers between devices with their start and end apart: 3, of which 3 were waited for; matrix products, arithmetic and copies ran while one was open for 0% of the time, Pallas kernels for 0%

profile of v1, /device:TPU:1, one launch (start us, length us, event | category | flops | bytes accessed | tf_op | source)
XLA Modules:
  0.0 269.9 jit_solution(14714945664040734543)
XLA Ops:
  6.5 0.7 all-gather.4.cloned.1.call-update
  8.0 69.7 %all-gather.4.cloned.1.call-done = bf16[256,3840]{0,1:T(8,128)(2,1)} async-done(((bf16[256,240]{0,1:T(8,128)(2,1)}), bf16[256,3840]{0,1:T(8,128)(2,1)}) %all-gather.4.cloned.1.call-update) | async-done | bytes 1966096 | tf_op jit(solution)/shard_map/all_gather | solution.py:16
  77.7 67.8 %while.11 = (s32[]{:T(128)}, f32[16,128,256]{2,0,1:T(8,128)}, s32[4]{0:T(128)S(1)}, s32[240]{0:T(256)}, pred[240]{0:T(512)(128)(4,1)S(1)}, /*index=5*/bf16[240,6...) while((s32[]{:T(128)}, f32[16,128,256]{2,0,1:T(8,128)}, ...), condition=%wide.region_1.2_spmd.clone, body=%wide.region_0.1_spmd.clone.sunk | while | flops 631180544 | bytes 43587780 | solution.py:40
  77.7 0.6 dynamic_slice.30
  79.0 0.8 dynamic_slice.31
  79.7 0.8 compare_and_fusion.2
  80.5 2.2 gather_fusion
  82.8 2.6 fusion.28
  85.4 7.9 %select_add_fusion.2 = f32[16,128,256]{2,0,1:T(8,128)S(1)} fusion(f32[16,128,256]{2,0,1:T(8,128)S(1)} %copy-done, f32[60,128,256]{2,1,0:T(8,128)S(1)} %fusion.28, pred[]{:T(512)S(6)} %compare.3, s32[60]{0:T(128)S(1)} %dynamic_slice.31, pred[60]{0:T(512)(128)(4,1)S(1)} %dynamic_slice.32), kind=kOutput, calls=%fused_computation.4.clone.1 | convolution fusion | flops 378537856 | bytes 12058925 | tf_op jit(solution)/shard_map/while/body/eval_jaxpr/ndq,nb->bdq/dot_general | solution.py:36
  93.3 1.3 copy-done.1
  95.9 0.8 dynamic_slice.31
  96.7 0.8 compare_and_fusion.2
  97.5 2.2 gather_fusion
  99.7 2.6 fusion.28
  102.3 7.9 %select_add_fusion.2 = f32[16,128,256]{2,0,1:T(8,128)S(1)} fusion(f32[16,128,256]{2,0,1:T(8,128)S(1)} %copy-done, f32[60,128,256]{2,1,0:T(8,128)S(1)} %fusion.28, pred[]{:T(512)S(6)} %compare.3, s32[60]{0:T(128)S(1)} %dynamic_slice.31, pred[60]{0:T(512)(128)(4,1)S(1)} %dynamic_slice.32), kind=kOutput, calls=%fused_computation.4.clone.1 | convolution fusion | flops 378537856 | bytes 12058925 | tf_op jit(solution)/shard_map/while/body/eval_jaxpr/ndq,nb->bdq/dot_general | solution.py:36
  110.2 1.3 copy-done.1
  112.9 0.8 dynamic_slice.31
  113.6 0.8 compare_and_fusion.2
  114.4 2.2 gather_fusion
  116.6 2.6 fusion.28
  119.3 7.9 %select_add_fusion.2 = f32[16,128,256]{2,0,1:T(8,128)S(1)} fusion(f32[16,128,256]{2,0,1:T(8,128)S(1)} %copy-done, f32[60,128,256]{2,1,0:T(8,128)S(1)} %fusion.28, pred[]{:T(512)S(6)} %compare.3, s32[60]{0:T(128)S(1)} %dynamic_slice.31, pred[60]{0:T(512)(128)(4,1)S(1)} %dynamic_slice.32), kind=kOutput, calls=%fused_computation.4.clone.1 | convolution fusion | flops 378537856 | bytes 12058925 | tf_op jit(solution)/shard_map/while/body/eval_jaxpr/ndq,nb->bdq/dot_general | solution.py:36
  127.2 1.3 copy-done.1
  129.8 0.8 dynamic_slice.31
  130.6 0.8 compare_and_fusion.2
  131.3 2.2 gather_fusion
  133.6 2.6 fusion.28
  136.2 7.9 %select_add_fusion.2 = f32[16,128,256]{2,0,1:T(8,128)S(1)} fusion(f32[16,128,256]{2,0,1:T(8,128)S(1)} %copy-done, f32[60,128,256]{2,1,0:T(8,128)S(1)} %fusion.28, pred[]{:T(512)S(6)} %compare.3, s32[60]{0:T(128)S(1)} %dynamic_slice.31, pred[60]{0:T(512)(128)(4,1)S(1)} %dynamic_slice.32), kind=kOutput, calls=%fused_computation.4.clone.1 | convolution fusion | flops 378537856 | bytes 12058925 | tf_op jit(solution)/shard_map/while/body/eval_jaxpr/ndq,nb->bdq/dot_general | solution.py:36
  144.1 1.3 copy-done.1
  145.5 4.1 %copy.7 = f32[16,128,256]{2,1,0:T(8,128)} copy(f32[16,128,256]{2,0,1:T(8,128)} %get-tuple-element.52) | data formatting | bytes 4194304 | tf_op jit(solution)/shard_map/while | solution.py:40
  149.6 69.9 %reduce-scatter.2.cloned.1.call-done = f32[128,256]{1,0:T(8,128)} async-done(((f32[2048,256]{1,0:T(8,128)}), f32[128,256]{1,0:T(8,128)}) %reduce-scatter.2.cloned.1.call-update) | async-done | bytes 131088 | tf_op jit(solution)/shard_map/reduce_scatter | solution.py:42
  219.6 41.8 %all-gather.6.cloned.1.call-done = f32[1024,256]{1,0:T(8,128)} async-done(((f32[128,256]{1,0:T(8,128)}), f32[1024,256]{1,0:T(8,128)}) %all-gather.6.cloned.1.call-update) | async-done | bytes 1048592 | tf_op jit(solution)/shard_map/all_gather | solution.py:43
  261.4 2.0 reduce_sum.9
  (31 shorter events, 2.3 us)
Async XLA Ops:
  6.5 71.2 %all-gather.4.cloned.1.call-start = ((), (), s32[]{:S(2)}) async-start(), calls=%async_computation.1 | async-start | bytes 2088960 | tf_op jit(solution)/shard_map/all_gather | solution.py:16
  7.3 212.3 %reduce-scatter.2.cloned.1.call-start = ((), (), s32[]{:S(2)}) async-start(), calls=%async_computation.2 | async-start | bytes 2228224 | tf_op jit(solution)/shard_map/reduce_scatter | solution.py:42
  82.7 2.6 copy-start
  93.3 1.3 copy-start.1
  99.7 2.6 copy-start
  110.2 1.3 copy-start.1
  116.6 2.6 copy-start
  127.2 1.3 copy-start.1
  133.6 2.6 copy-start
  144.1 1.3 copy-start.1
  149.6 111.8 %all-gather.6.cloned.1.call-start = ((), (), s32[]{:S(2)}) async-start(), calls=%async_computation.3 | async-start | bytes 1179648 | tf_op jit(solution)/shard_map/all_gather | solution.py:43
Sparse Core Ops, SparseCore 0:
  9.4 68.2 all-gather.3
  149.7 69.8 reduce-scatter.1
  221.7 39.6 all-gather.5
